TPU v7x, 32 devices: a whole 2x2x4 slice. The times are simulated.
32 devices in a mesh: fsdp: 4 (over y, core), ctx: 2 (over x), tp: 4 (over z).
Axes of the slice: x: 2, y: 2, z: 4, core: 2. Of those that a mesh axis runs over, the one named last changes fastest.
Arguments:
- tokens: bfloat16 [4, 1024, 2048], P('fsdp', 'ctx'), may hold values from -6 to 6
- lengths: int32 [4, 3], P('fsdp'), may hold values from 1 to 768, 960 in all within a row
- block_order: int32 [4, 4], P('fsdp'), may hold values from 0 to 3, each once within a row
- ln_gain: bfloat16 [2048], P('fsdp'), may hold values from 0.25 to 1.75
- ln_bias: bfloat16 [2048], P('fsdp'), may hold values from -3 to 3
- qkv_weight: bfloat16 [2048, 3, 2048], P('fsdp', None, 'tp'), may hold values from -0.125 to 0.125
- qkv_bias: bfloat16 [3, 2048], P(None, 'tp'), may hold values from -0.59765625 to 0.59765625
- dense_weight: bfloat16 [2048, 2048], P('fsdp', 'tp'), may hold values from -1 to 1
- dense_bias: bfloat16 [2048], P('fsdp'), may hold values from -3 to 3
- fc1_weight: bfloat16 [2048, 8192], P('fsdp', 'tp'), may hold values from -0.125 to 0.125
- fc1_bias: bfloat16 [8192], P('tp'), may hold values from -3 to 3
- fc2_weight: bfloat16 [2048, 8192], P('fsdp', 'tp'), may hold values from -0.0625 to 0.0625
- fc2_bias: bfloat16 [2048], P('fsdp'), may hold values from -3 to 3
- cotangent: bfloat16 [4, 1024, 2048], P('fsdp', 'ctx'), may hold values from -6 to 6
Outputs:
- output: bfloat16 [4, 1024, 2048], P('fsdp', 'ctx')
- input_grad: float32 [4, 1024, 2048], P('fsdp', 'ctx')
- ln_gain_grad: float32 [2048], P('fsdp')
- ln_bias_grad: float32 [2048], P('fsdp')
- qkv_weight_grad: float32 [2048, 3, 2048], P('fsdp', None, 'tp')
- qkv_bias_grad: float32 [3, 2048], P(None, 'tp')
- dense_weight_grad: float32 [2048, 2048], P('fsdp', 'tp')
- dense_bias_grad: float32 [2048], P('fsdp')
- fc1_weight_grad: float32 [2048, 8192], P('fsdp', 'tp')
- fc1_bias_grad: float32 [8192], P('tp')
- fc2_weight_grad: float32 [2048, 8192], P('fsdp', 'tp')
- fc2_bias_grad: float32 [2048], P('fsdp')
Inputs may be any that keep to these rules, and one draw needn't show every extreme that they name: Each row holds the lengths of 3 sequences packed from the row's start; they sum to 960 and the largest is exactly 768. Each row is a permutation of the 4 block numbers; dealt block j holds packed block block_order[b, j].
All inputs are finite; a program needn't handle non-finite values.
Results may differ from a plain program's by a relative error of at most 0.012.
Values may be sent and summed in bfloat16 or wider, within the bound.
No kernel may reach another device: no remote copies, remote signals or barrier semaphores. Data moves between devices by JAX's collectives and lax.ppermute only.
A program may use at most 256 MiB of HBM per device.

v0:
```python
import math
import jax
import jax.numpy as jnp
from jax import lax
from jax.sharding import PartitionSpec as P

HD = 256
ROT = 64
NORM_EPSILON = 1e-05
MASK_FLOOR = -1000000000.0


def rotation_tables(position):
    frequency = jnp.exp(jnp.arange(ROT // 2, dtype=jnp.float32) * (-2.0 * math.log(10000.0) / ROT))
    angles = position.astype(jnp.float32)[:, None] * frequency[None, :]
    return (jnp.cos(angles)[:, None, :], jnp.sin(angles)[:, None, :])


def rotate(values, cosine_table, sine_table):
    first_half = values[..., : ROT // 2]
    second_half = values[..., ROT // 2 : ROT]
    return jnp.concatenate(
        [
            first_half * cosine_table - second_half * sine_table,
            second_half * cosine_table + first_half * sine_table,
            values[..., ROT:],
        ],
        axis=-1,
    )


def rotate_back(grads, cosine_table, sine_table):
    first_half = grads[..., : ROT // 2]
    second_half = grads[..., ROT // 2 : ROT]
    return jnp.concatenate(
        [
            first_half * cosine_table + second_half * sine_table,
            second_half * cosine_table - first_half * sine_table,
            grads[..., ROT:],
        ],
        axis=-1,
    )


def packed_rows(order_row, first_slot, row_count, block_rows):
    row_index = jnp.arange(row_count, dtype=jnp.int32)
    dealt_slot = first_slot + row_index // block_rows
    selector = dealt_slot[:, None] == jnp.arange(order_row.shape[0], dtype=jnp.int32)[None, :]
    source_block = jnp.sum(jnp.where(selector, order_row[None, :], 0), axis=1, dtype=jnp.int32)
    return source_block * block_rows + row_index % block_rows


def place_rows(packed_at, lengths_row):
    seq_ends = jnp.cumsum(lengths_row, dtype=jnp.int32)
    passed = packed_at[:, None] >= seq_ends[None, :]
    segment = jnp.sum(passed.astype(jnp.int32), axis=1, dtype=jnp.int32)
    before = jnp.sum(jnp.where(passed, lengths_row[None, :], 0), axis=1, dtype=jnp.int32)
    return (segment, packed_at - before)


def gelu_slope(value):
    normal_cdf = 0.5 * (1.0 + lax.erf(value * (1.0 / math.sqrt(2.0))))
    density = jnp.exp(-0.5 * value * value) * (1.0 / math.sqrt(2.0 * math.pi))
    return normal_cdf + value * density


def per_device(
    tokens,
    lengths,
    block_order,
    ln_gain,
    ln_bias,
    qkv_weight,
    qkv_bias,
    dense_weight,
    dense_bias,
    fc1_weight,
    fc1_bias,
    fc2_weight,
    fc2_bias,
    cotangent,
):
    gathered = (
        lax.all_gather(qkv_weight, "fsdp", axis=0, tiled=True),
        lax.all_gather(dense_weight, "fsdp", axis=0, tiled=True),
        lax.all_gather(fc1_weight, "fsdp", axis=0, tiled=True),
        lax.all_gather(fc2_weight, "fsdp", axis=0, tiled=True),
        lax.all_gather(ln_gain, "fsdp", axis=0, tiled=True),
        lax.all_gather(ln_bias, "fsdp", axis=0, tiled=True),
        lax.all_gather(dense_bias, "fsdp", axis=0, tiled=True),
        lax.all_gather(fc2_bias, "fsdp", axis=0, tiled=True),
    )
    qkv_full = gathered[0]
    dense_full = gathered[1]
    fc1_full = gathered[2]
    fc2_full = gathered[3]
    norm_gain = gathered[4].astype(jnp.float32)
    norm_bias = gathered[5].astype(jnp.float32)
    out_bias = gathered[6].astype(jnp.float32) + gathered[7].astype(jnp.float32)
    inputs = tokens[0].astype(jnp.float32)
    row_count = inputs.shape[0]
    block_rows = row_count // 2
    group_rows = row_count * lax.axis_size("ctx")
    lengths_row = lengths[0]
    order_row = block_order[0]
    seq_count = lengths_row.shape[0]
    local_packed = packed_rows(order_row, lax.axis_index("ctx") * 2, row_count, block_rows)
    key_packed = packed_rows(order_row, 0, group_rows, block_rows)
    local_segment, local_position = place_rows(local_packed, lengths_row)
    key_segment = place_rows(key_packed, lengths_row)[0]
    valid_rows = (local_segment < seq_count).astype(jnp.float32)
    allowed = (local_segment[:, None] == key_segment[None, :]) & (
        key_packed[None, :] <= local_packed[:, None]
    )
    cosine_table, sine_table = rotation_tables(local_position)
    score_scale = 1.0 / math.sqrt(HD)
    row_mean = jnp.mean(inputs, axis=1, keepdims=True)
    centred = inputs - row_mean
    variance = jnp.mean(centred * centred, axis=1, keepdims=True)
    inverse = lax.rsqrt(variance + NORM_EPSILON)
    standard = centred * inverse
    normed = (standard * norm_gain + norm_bias).astype(jnp.bfloat16)
    projected = jnp.einsum(
        "td,dce->tce", normed, qkv_full, preferred_element_type=jnp.float32
    ) + qkv_bias.astype(jnp.float32)
    heads_here = projected.shape[2] // HD
    shaped = projected.reshape(row_count, 3, heads_here, HD)
    queries = rotate(shaped[:, 0], cosine_table, sine_table).astype(jnp.bfloat16)
    keys_local = rotate(shaped[:, 1], cosine_table, sine_table).astype(jnp.bfloat16)
    values_local = shaped[:, 2].astype(jnp.bfloat16)
    keys_all, values_all = (
        lax.all_gather(keys_local, "ctx", axis=0, tiled=True),
        lax.all_gather(values_local, "ctx", axis=0, tiled=True),
    )

    def head_scores(head_index):
        scores = (
            jnp.einsum(
                "qe,ke->qk",
                queries[:, head_index],
                keys_all[:, head_index],
                preferred_element_type=jnp.float32,
            )
            * score_scale
        )
        return jnp.where(allowed, scores, MASK_FLOOR)

    head_outputs = []
    log_totals = []
    for head_index in range(heads_here):
        scores = head_scores(head_index)
        row_max = jnp.max(scores, axis=1, keepdims=True)
        exp_scores = jnp.exp(scores - row_max)
        row_total = jnp.sum(exp_scores, axis=1, keepdims=True)
        probabilities = (exp_scores / row_total).astype(jnp.bfloat16)
        head_outputs.append(
            jnp.dot(probabilities, values_all[:, head_index], preferred_element_type=jnp.float32)
        )
        log_totals.append(row_max + jnp.log(row_total))
    attended = (
        (jnp.stack(head_outputs, axis=1) * valid_rows[:, None, None])
        .astype(jnp.bfloat16)
        .reshape(row_count, heads_here * HD)
    )
    pre_act = jnp.dot(normed, fc1_full, preferred_element_type=jnp.float32) + fc1_bias.astype(
        jnp.float32
    )
    hidden = jax.nn.gelu(pre_act, approximate=False).astype(jnp.bfloat16)
    partial_out = jnp.einsum(
        "te,de->td", attended, dense_full, preferred_element_type=jnp.float32
    ) + jnp.einsum("tf,df->td", hidden, fc2_full, preferred_element_type=jnp.float32)
    summed = lax.psum(partial_out, "tp")
    output = (inputs + summed + out_bias).astype(jnp.bfloat16)
    upstream_low = cotangent[0]
    upstream = upstream_low.astype(jnp.float32)
    out_bias_grad = jnp.sum(upstream, axis=0)
    dense_grad = jnp.einsum("td,te->de", upstream_low, attended, preferred_element_type=jnp.float32)
    fc2_grad = jnp.einsum("td,tf->df", upstream_low, hidden, preferred_element_type=jnp.float32)
    attended_grad = (
        jnp.dot(upstream_low, dense_full, preferred_element_type=jnp.float32).astype(jnp.bfloat16)
        * valid_rows[:, None].astype(jnp.bfloat16)
    ).reshape(row_count, heads_here, HD)
    hidden_grad = jnp.dot(upstream_low, fc2_full, preferred_element_type=jnp.float32)
    pre_grad = (hidden_grad * gelu_slope(pre_act)).astype(jnp.bfloat16)
    fc1_bias_grad = jnp.sum(pre_grad.astype(jnp.float32), axis=0)
    fc1_grad = jnp.einsum("td,tf->df", normed, pre_grad, preferred_element_type=jnp.float32)
    normed_grad = jnp.einsum("tf,df->td", pre_grad, fc1_full, preferred_element_type=jnp.float32)
    query_pieces = []
    key_pieces = []
    value_pieces = []
    for head_index in range(heads_here):
        probs_full = jnp.exp(head_scores(head_index) - log_totals[head_index])
        probs_low = probs_full.astype(jnp.bfloat16)
        head_grad = attended_grad[:, head_index]
        prob_grad = jnp.einsum(
            "qe,ke->qk", head_grad, values_all[:, head_index], preferred_element_type=jnp.float32
        )
        row_delta = jnp.sum(probs_full * prob_grad, axis=1, keepdims=True)
        score_grad = (probs_full * (prob_grad - row_delta)).astype(jnp.bfloat16)
        query_pieces.append(
            jnp.dot(score_grad, keys_all[:, head_index], preferred_element_type=jnp.float32)
            * score_scale
        )
        key_pieces.append(
            jnp.einsum(
                "qk,qe->ke", score_grad, queries[:, head_index], preferred_element_type=jnp.float32
            )
            * score_scale
        )
        value_pieces.append(
            jnp.einsum("qk,qe->ke", probs_low, head_grad, preferred_element_type=jnp.float32)
        )
    own_keys, own_values = (
        lax.psum_scatter(jnp.stack(key_pieces, axis=1), "ctx", scatter_dimension=0, tiled=True),
        lax.psum_scatter(jnp.stack(value_pieces, axis=1), "ctx", scatter_dimension=0, tiled=True),
    )
    query_turned = rotate_back(jnp.stack(query_pieces, axis=1), cosine_table, sine_table)
    key_turned = rotate_back(own_keys, cosine_table, sine_table)
    proj_grad = (
        jnp.stack([query_turned, key_turned, own_values], axis=1)
        .astype(jnp.bfloat16)
        .reshape(row_count, 3, heads_here * HD)
    )
    qkv_bias_grad = jnp.sum(proj_grad.astype(jnp.float32), axis=0)
    qkv_grad = jnp.einsum("td,tce->dce", normed, proj_grad, preferred_element_type=jnp.float32)
    normed_grad = normed_grad + jnp.einsum(
        "tce,dce->td", proj_grad, qkv_full, preferred_element_type=jnp.float32
    )
    full_grad = lax.psum(normed_grad, "tp")
    gain_grad = jnp.sum(full_grad * standard, axis=0)
    shift_grad = jnp.sum(full_grad, axis=0)
    scaled = full_grad * norm_gain
    input_grad = upstream + inverse * (
        scaled
        - jnp.mean(scaled, axis=1, keepdims=True)
        - standard * jnp.mean(scaled * standard, axis=1, keepdims=True)
    )
    bias_sums = lax.psum((qkv_bias_grad, fc1_bias_grad), ("fsdp", "ctx"))
    reduced = (
        lax.psum_scatter(qkv_grad, ("fsdp", "ctx"), scatter_dimension=0, tiled=True),
        lax.psum_scatter(dense_grad, ("fsdp", "ctx"), scatter_dimension=0, tiled=True),
        lax.psum_scatter(fc1_grad, ("fsdp", "ctx"), scatter_dimension=0, tiled=True),
        lax.psum_scatter(fc2_grad, ("fsdp", "ctx"), scatter_dimension=0, tiled=True),
        lax.psum_scatter(gain_grad, ("fsdp", "ctx"), scatter_dimension=0, tiled=True),
        lax.psum_scatter(shift_grad, ("fsdp", "ctx"), scatter_dimension=0, tiled=True),
        lax.psum_scatter(out_bias_grad, ("fsdp", "ctx"), scatter_dimension=0, tiled=True),
    )
    shards = (
        lax.all_gather(reduced[0], "ctx", axis=0, tiled=True),
        lax.all_gather(reduced[1], "ctx", axis=0, tiled=True),
        lax.all_gather(reduced[2], "ctx", axis=0, tiled=True),
        lax.all_gather(reduced[3], "ctx", axis=0, tiled=True),
        lax.all_gather(reduced[4], "ctx", axis=0, tiled=True),
        lax.all_gather(reduced[5], "ctx", axis=0, tiled=True),
        lax.all_gather(reduced[6], "ctx", axis=0, tiled=True),
    )
    return (
        output[None],
        input_grad[None],
        shards[4],
        shards[5],
        shards[0],
        bias_sums[0],
        shards[1],
        shards[6],
        shards[2],
        bias_sums[1],
        shards[3],
        shards[6],
    )


def solution(mesh):
    placed = (
        P("fsdp", "ctx", None),
        P("fsdp", None),
        P("fsdp", None),
        P("fsdp"),
        P("fsdp"),
        P("fsdp", None, "tp"),
        P(None, "tp"),
        P("fsdp", "tp"),
        P("fsdp"),
        P("fsdp", "tp"),
        P("tp"),
        P("fsdp", "tp"),
        P("fsdp"),
        P("fsdp", "ctx", None),
    )
    return jax.shard_map(
        per_device,
        mesh=mesh,
        in_specs=placed,
        out_specs=(
            P("fsdp", "ctx", None),
            P("fsdp", "ctx", None),
            P("fsdp"),
            P("fsdp"),
            P("fsdp", None, "tp"),
            P(None, "tp"),
            P("fsdp", "tp"),
            P("fsdp"),
            P("fsdp", "tp"),
            P("tp"),
            P("fsdp", "tp"),
            P("fsdp"),
        ),
        check_vma=False,
    )
```

profile of v0, /device:TPU:0, one launch (start us, length us, event | category | flops | bytes accessed | tf_op | source)
XLA Modules:
  0.0 1210.0 jit_solution(16124537954326559841)
XLA Ops:
  7.3 2.7 copy.57
  11.0 6.2 all-gather.2
  17.2 5.5 all-gather.1
  24.5 34.9 %all-gather.19.cloned.1.call-done = bf16[2048,3,512]{0,2,1:T(8,128)(2,1)} async-done(((bf16[512,3,512]{0,2,1:T(8,128)(2,1)}), bf16[2048,3,512]{0,2,1:T(8,128)(2,1)}) %all-gather.19.cloned.1.call-update) | async-done | bytes 6291472 | tf_op jit(solution)/shard_map/all_gather | solution.py:84
  59.3 5.9 fusion.46
  69.2 14.3 %all-gather.23.cloned.1.call-done = bf16[2048,512]{1,0:T(8,128)(2,1)} async-done(((bf16[512,512]{1,0:T(8,128)(2,1)}), bf16[2048,512]{1,0:T(8,128)(2,1)}) %all-gather.23.cloned.1.call-update) | async-done | bytes 2097168 | tf_op jit(solution)/shard_map/all_gather | solution.py:85
  83.5 4.3 fusion.58
  87.8 2.1 slice.201
  90.9 16.0 %all-gather.21.cloned.1.call-done = bf16[1024,2,256]{0,2,1:T(8,128)(2,1)} async-done(((bf16[512,2,256]{0,2,1:T(8,128)(2,1)}), bf16[1024,2,256]{0,2,1:T(8,128)(2,1)}) %all-gather.21.cloned.1.call-update) | async-done | bytes 1048592 | tf_op jit(solution)/shard_map/all_gather | solution.py:132
  114.5 15.7 %all-gather.37.cloned.1.call-done = bf16[1024,1,2,256]{0,3,2,1:T(8,128)(2,1)} async-done(((bf16[512,1,2,256]{0,3,2,1:T(8,128)(2,1)}), bf16[1024,1,2,256]{0,3,2,1:T(8,128)(2,1)}) %all-gather.37.cloned.1.call-update) | async-done | bytes 1048592 | tf_op jit(solution)/shard_map/all_gather | solution.py:133
  130.2 2.5 multiply_reduce_fusion.2
  140.1 2.4 convolution_bitcast_fusion.4
  144.2 3.3 convolution_bitcast_fusion.1
  152.3 12.5 %reduce-scatter.9.cloned.1.call-done = f32[512,2,256]{2,0,1:T(8,128)} async-done(((f32[1024,2,256]{2,0,1:T(8,128)}), f32[512,2,256]{2,0,1:T(8,128)}) %reduce-scatter.9.cloned.1.call-update) | async-done | bytes 1048592 | tf_op jit(solution)/shard_map/reduce_scatter | solution.py:215
  164.9 2.1 convert.64
  169.0 2.1 copy.63
  171.0 28.4 %reduce-scatter.7.cloned.1.call-done = f32[512,2,256]{0,2,1:T(8,128)} async-done(((f32[1024,2,256]{0,2,1:T(8,128)}), f32[512,2,256]{0,2,1:T(8,128)}) %reduce-scatter.7.cloned.1.call-update) | async-done | bytes 1048592 | tf_op jit(solution)/shard_map/reduce_scatter | solution.py:214
  203.1 2.1 copy.61
  205.1 2.1 copy.62
  207.2 8.8 fusion.40
  216.7 42.6 %all-gather.25.cloned.1.call-done = bf16[2048,2048]{1,0:T(8,128)(2,1)} async-done(((bf16[512,2048]{1,0:T(8,128)(2,1)}), bf16[2048,2048]{1,0:T(8,128)(2,1)}) %all-gather.25.cloned.1.call-update) | async-done | bytes 8388624 | tf_op jit(solution)/shard_map/all_gather | solution.py:86
  259.3 17.2 %fusion.20 = (bf16[512,2048]{1,0:T(8,128)(2,1)}, f32[512,2048]{1,0:T(8,128)}) fusion(f32[2048]{0:T(1024)S(1)} %convert_element_type.135, bf16[2048,2048]{1,0:T(8,128)(2,1)} %all-gather.25.cloned.1.call-done, bf16[1,512,2048]{2,1,0:T(8,128)(2,1)S(1)} %copy-done, f32[2048]{0:T(1024)S(1)} %bitcast.223, f32[2048]{0:T(1024)S(1)} %bitcast.214, ...), kind=kOutput, calls=%fused_computation.27 | convolution fusion | flops 4370464768 | bytes 16805888 | tf_op jit(solution)/shard_map/dot_general | solution.py:165
  276.5 42.7 %all-gather.27.cloned.1.call-done = bf16[2048,2048]{1,0:T(8,128)(2,1)} async-done(((bf16[512,2048]{1,0:T(8,128)(2,1)}), bf16[2048,2048]{1,0:T(8,128)(2,1)}) %all-gather.27.cloned.1.call-update) | async-done | bytes 8388624 | tf_op jit(solution)/shard_map/all_gather | solution.py:87
  319.2 9.4 convert_reduce_fusion.2
  329.9 8.8 fusion.92
  339.2 12.5 %convolution_bitcast_fusion = f32[2048,2048]{0,1:T(8,128)} fusion(bf16[512,2048]{1,0:T(8,128)(2,1)} %get-tuple-element.96, bf16[1,512,2048]{2,1,0:T(8,128)(2,1)} %param.27), kind=kOutput, calls=%fused_computation | convolution fusion | flops 4294967296 | bytes 20971520 | tf_op jit(solution)/shard_map/td,tf->df/dot_general | solution.py:178
  353.3 10.8 fusion.99
  364.1 9.8 fusion.100
  374.5 6.5 convolution_add_fusion
  381.0 8.7 bitcast_add_fusion
  389.8 79.9 %reduce-scatter.11.cloned.1.call-done = f32[256,3,512]{2,0,1:T(8,128)} async-done(((f32[2048,3,512]{2,0,1:T(8,128)}), f32[256,3,512]{2,0,1:T(8,128)}) %reduce-scatter.11.cloned.1.call-update) | async-done | bytes 1572880 | tf_op jit(solution)/shard_map/reduce_scatter | solution.py:240
  469.7 119.7 %reduce-scatter.15.cloned.1.call-done = f32[256,2048]{1,0:T(8,128)} async-done(((f32[2048,2048]{1,0:T(8,128)}), f32[256,2048]{1,0:T(8,128)}) %reduce-scatter.15.cloned.1.call-update) | async-done | bytes 2097168 | tf_op jit(solution)/shard_map/reduce_scatter | solution.py:242
  589.5 119.4 %reduce-scatter.17.cloned.1.call-done = f32[256,2048]{0,1:T(8,128)} async-done(((f32[2048,2048]{0,1:T(8,128)}), f32[256,2048]{0,1:T(8,128)}) %reduce-scatter.17.cloned.1.call-update) | async-done | bytes 2097168 | tf_op jit(solution)/shard_map/reduce_scatter | solution.py:243
  710.2 5.2 all-gather.4
  715.4 5.2 all-gather.3
  721.9 9.8 all-gather.31.cloned.1.call-done
  731.8 2.5 copy.66
  734.3 291.4 %all-reduce.7.cloned.1.call-done = (f32[512,2048]{1,0:T(8,128)}, f32[512,2048]{1,0:T(8,128)}) async-done(((f32[512,2048]{1,0:T(8,128)}, f32[512,2048]{1,0:T(8,128)}), (f32[512,2048]{1,0:T(8,128)}, f32[512,2048]{1,0:T(8,128)})) %all-reduce.7.cloned.1.call-update) | async-done | bytes 8388624 | tf_op jit(solution)/shard_map/psum | solution.py:172
  1025.7 3.9 fusion.13
  1029.8 6.1 convert_reduce_fusion
  1035.8 28.5 %all-reduce.3 = (f32[2048]{0:T(1024)S(1)}, f32[2048]{0:T(1024)S(1)}, f32[3,512]{1,0:T(4,128)}, f32[2048]{0:T(1024)S(1)}, f32[2048]{0:T(1024)}) all-reduce(f32[2048]{0:T(1024)S(1)} %get-tuple-element.60, f32[2048]{0:T(1024)S(1)} %get-tuple-element.63, ...), channel_id=5, replica_groups=mesh['fsdp'=4,'ctx'=2,'tp'=4] {'fsdp','ctx'}, use_global_device_ids=true, to_apply=%region_21.22.clone | all-reduce | flops 9728 | bytes 77824
  1064.4 4.4 all-gather.7
  1068.9 4.3 all-gather.5
  1073.2 4.2 all-gather.6
  1077.5 54.2 %all-gather.33.cloned.1.call-done = f32[512,2048]{1,0:T(8,128)} async-done(((f32[256,2048]{1,0:T(8,128)}), f32[512,2048]{1,0:T(8,128)}) %all-gather.33.cloned.1.call-update) | async-done | bytes 4194320 | tf_op jit(solution)/shard_map/all_gather | solution.py:251
  1131.6 58.1 %all-gather.35.cloned.1.call-done = f32[512,2048]{0,1:T(8,128)} async-done(((f32[256,2048]{0,1:T(8,128)}), f32[512,2048]{0,1:T(8,128)}) %all-gather.35.cloned.1.call-update) | async-done | bytes 4194320 | tf_op jit(solution)/shard_map/all_gather | solution.py:252
  1189.8 5.3 copy.67
  1196.9 3.9 copy.84
  (191 shorter events, 45.9 us)
Async XLA Ops:
  7.2 3.7 copy-start.32
  7.2 3.8 copy-start.33
  7.2 3.8 copy-start.34
  7.2 15.5 %copy-start.30 = (bf16[3,512]{1,0:T(4,128)(2,1)S(1)}, bf16[3,512]{1,0:T(4,128)(2,1)}, u32[]{:S(2)}) copy-start(bf16[3,512]{1,0:T(4,128)(2,1)} %param.20) | copy-start | bytes 9220
  7.2 15.5 %copy-start.37 = (s32[1,3]{1,0:T(1,128)S(1)}, s32[1,3]{1,0:T(1,128)}, u32[]{:S(2)}) copy-start(s32[1,3]{1,0:T(1,128)} %param.15) | copy-start | bytes 40
  7.2 15.8 %copy-start = (bf16[1,512,2048]{2,1,0:T(8,128)(2,1)S(1)}, bf16[1,512,2048]{2,1,0:T(8,128)(2,1)}, u32[]{:S(2)}) copy-start(bf16[1,512,2048]{2,1,0:T(8,128)(2,1)} %param.14) | copy-start | bytes 6291460
  7.2 52.1 %all-gather.19.cloned.1.call-start = ((), (), s32[]{:S(2)}) async-start(), calls=%async_computation.6 | async-start | bytes 7864320 | tf_op jit(solution)/shard_map/all_gather | solution.py:84
  10.0 73.5 %all-gather.23.cloned.1.call-start = ((), (), s32[]{:S(2)}) async-start(), calls=%async_computation.8 | async-start | bytes 2621440 | tf_op jit(solution)/shard_map/all_gather | solution.py:85
  10.8 96.1 %all-gather.21.cloned.1.call-start = ((), (), s32[]{:S(2)}) async-start(), calls=%async_computation.7 | async-start | bytes 1572864 | tf_op jit(solution)/shard_map/all_gather | solution.py:132
  11.0 12.1 copy-start.26
  17.2 48.0 %copy-start.28 = (f32[4,1,512]{2,1,0:T(1,128)}, f32[4,1,512]{2,1,0:T(1,128)S(1)}, u32[]{:S(2)}) copy-start(f32[4,1,512]{2,1,0:T(1,128)S(1)} %convert_element_type.153) | copy-start | bytes 24580
  23.0 45.6 %copy-start.27 = (s32[512]{0:T(512)}, s32[512]{0:T(512)S(1)}, u32[]{:S(2)}) copy-start(s32[512]{0:T(512)S(1)} %get-tuple-element.65) | copy-start | bytes 6148
  24.5 41.1 %copy-start.21 = (f32[512,32]{0,1:T(8,128)}, f32[512,32]{0,1:T(8,128)S(1)}, u32[]{:S(2)}) copy-start(f32[512,32]{0,1:T(8,128)S(1)} %get-tuple-element.92) | copy-start | bytes 196612
  24.5 41.1 %copy-start.22 = (f32[512,32]{0,1:T(8,128)}, f32[512,32]{0,1:T(8,128)S(1)}, u32[]{:S(2)}) copy-start(f32[512,32]{0,1:T(8,128)S(1)} %get-tuple-element.93) | copy-start | bytes 196612
  67.8 62.4 %all-gather.37.cloned.1.call-start = ((), (), s32[]{:S(2)}) async-start(), calls=%async_computation.21 | async-start | bytes 1572864 | tf_op jit(solution)/shard_map/all_gather | solution.py:133
  68.0 19.8 %copy-start.25 = (s32[1024]{0:T(1024)}, s32[1024]{0:T(1024)S(1)}, u32[]{:S(2)}) copy-start(s32[1024]{0:T(1024)S(1)} %fusion.79) | copy-start | bytes 12292
  90.0 74.9 %reduce-scatter.9.cloned.1.call-start = ((), (), s32[]{:S(2)}) async-start(), calls=%async_computation.12 | async-start | bytes 3145728 | tf_op jit(solution)/shard_map/reduce_scatter | solution.py:215
  106.9 2.4 copy-start.38
  108.8 2.7 copy-start.1
  108.8 2.7 copy-start.13
  114.3 85.2 %reduce-scatter.7.cloned.1.call-start = ((), (), s32[]{:S(2)}) async-start(), calls=%async_computation.11 | async-start | bytes 3145728 | tf_op jit(solution)/shard_map/reduce_scatter | solution.py:214
  130.2 2.5 copy-start.4
  132.8 2.2 copy-start.19
  133.3 2.9 copy-start.10
  138.6 120.8 %all-gather.25.cloned.1.call-start = ((), (), s32[]{:S(2)}) async-start(), calls=%async_computation.9 | async-start | bytes 10485760 | tf_op jit(solution)/shard_map/all_gather | solution.py:86
  139.3 179.9 %all-gather.27.cloned.1.call-start = ((), (), s32[]{:S(2)}) async-start(), calls=%async_computation.10 | async-start | bytes 10485760 | tf_op jit(solution)/shard_map/all_gather | solution.py:87
  140.1 234.2 %reduce-scatter.13.cloned.1.call-start = ((), (), s32[]{:S(2)}) async-start(), calls=%async_computation.15 | async-start | bytes 4718592 | tf_op jit(solution)/shard_map/reduce_scatter | solution.py:241
  140.1 2.4 copy-start.5
  147.5 322.2 %reduce-scatter.11.cloned.1.call-start = ((), (), s32[]{:S(2)}) async-start(), calls=%async_computation.13 | async-start | bytes 14155776 | tf_op jit(solution)/shard_map/reduce_scatter | solution.py:240
  216.0 43.3 %copy-start.29 = (f32[4,1,512]{2,1,0:T(1,128)S(1)}, f32[4,1,512]{2,1,0:T(1,128)}, u32[]{:S(2)}) copy-start(f32[4,1,512]{2,1,0:T(1,128)} %copy-done.28) | copy-start | bytes 24580
  216.0 373.4 %reduce-scatter.15.cloned.1.call-start = ((), (), s32[]{:S(2)}) async-start(), calls=%async_computation.17 | async-start | bytes 18874368 | tf_op jit(solution)/shard_map/reduce_scatter | solution.py:242
  338.7 370.2 %reduce-scatter.17.cloned.1.call-start = ((), (), s32[]{:S(2)}) async-start(), calls=%async_computation.19 | async-start | bytes 18874368 | tf_op jit(solution)/shard_map/reduce_scatter | solution.py:243
  351.8 380.0 %all-gather.31.cloned.1.call-start = ((), (), s32[]{:S(2)}) async-start(), calls=%async_computation.16 | async-start | bytes 1572864 | tf_op jit(solution)/shard_map/all_gather | solution.py:250
  353.3 10.8 copy-start.42
  374.3 6.7 copy-start.14
  374.3 6.7 copy-start.15
  374.3 651.4 %all-reduce.7.cloned.1.call-start = ((), (), s32[]{:S(2)}) async-start(), calls=%async_computation.22 | async-start | bytes 16777216 | tf_op jit(solution)/shard_map/psum | solution.py:172
  374.5 6.5 copy-start.16
  374.5 6.5 copy-start.40
  389.7 319.2 %copy-start.35 = (bf16[512]{0:T(512)(128)(2,1)S(1)}, bf16[512]{0:T(512)(128)(2,1)}, u32[]{:S(2)}) copy-start(bf16[512]{0:T(512)(128)(2,1)} %param.22) | copy-start | bytes 3076
  389.8 319.2 %copy-start.36 = (bf16[512]{0:T(512)(128)(2,1)S(1)}, bf16[512]{0:T(512)(128)(2,1)}, u32[]{:S(2)}) copy-start(bf16[512]{0:T(512)(128)(2,1)} %param.26) | copy-start | bytes 3076
  389.8 319.2 %copy-start.39 = (u32[32]{0:T(128)S(1)}, u32[32]{0:T(128)}, u32[]{:S(2)}) copy-start(u32[32]{0:T(128)} %constant.160) | copy-start | bytes 388
  389.8 687.7 %all-gather.29.cloned.1.call-start = ((), (), s32[]{:S(2)}) async-start(), calls=%async_computation.14 | async-start | bytes 4718592 | tf_op jit(solution)/shard_map/all_gather | solution.py:249
  469.7 661.9 %all-gather.33.cloned.1.call-start = ((), (), s32[]{:S(2)}) async-start(), calls=%async_computation.18 | async-start | bytes 6291456 | tf_op jit(solution)/shard_map/all_gather | solution.py:251
  589.5 600.3 %all-gather.35.cloned.1.call-start = ((), (), s32[]{:S(2)}) async-start(), calls=%async_computation.20 | async-start | bytes 6291456 | tf_op jit(solution)/shard_map/all_gather | solution.py:252
  1025.7 3.9 copy-start.6
  1025.7 4.1 copy-start.8
  1195.1 6.2 copy-start.9
  (12 other events, 15.8 us)
Sparse Core Ops, SparseCore 0:
  10.2 49.1 all-gather.18
  60.9 22.5 all-gather.22
  85.6 21.2 all-gather.20
  108.9 21.2 all-gather.36
  132.9 31.9 reduce-scatter.8
  167.5 31.8 reduce-scatter.6
  201.0 58.2 all-gather.24
  260.9 58.2 all-gather.26
  323.1 51.0 reduce-scatter.12
  377.6 92.0 reduce-scatter.10
  473.2 116.1 reduce-scatter.14
  592.9 115.9 reduce-scatter.16
  710.4 21.2 all-gather.30
  734.8 290.8 all-reduce.6
  1027.0 46.3 all-gather.28
  1074.9 56.7 all-gather.32
  1133.0 56.7 all-gather.34
where the time goes:
time: 1220 us; the launch traced here: 1210 us
  waiting for transfers between devices  942 us (77%)
  matrix products  122 us (10%)
  blocking collectives  63.4 us (5%)
  local copies, waits for them, and re-layouts  37.8 us (3%)
  other arithmetic  27.6 us (2%)
  between operations  15.6 us (1%)
    psum x1, waiting for transfers between devices, per_device(): summed = lax.psum(partial_out, 'tp')  291 us
    reduce_scatter x1, waiting for transfers between devices, per_device(): lax.psum_scatter(fc1_grad, ('fsdp', 'ctx'), scatter_dimension=0, tiled=True)  120 us
    reduce_scatter x1, waiting for transfers between devices, per_device(): lax.psum_scatter(fc2_grad, ('fsdp', 'ctx'), scatter_dimension=0, tiled=True)  119 us
    reduce_scatter x1, waiting for transfers between devices, per_device(): lax.psum_scatter(qkv_grad, ('fsdp', 'ctx'), scatter_dimension=0, tiled=True)  79.9 us
    all_gather x1, waiting for transfers between devices, per_device(): lax.all_gather(reduced[3], 'ctx', axis=0, tiled=True)  58.1 us
    all_gather x1, waiting for transfers between devices, per_device(): lax.all_gather(reduced[2], 'ctx', axis=0, tiled=True)  54.2 us
    all_gather x1, waiting for transfers between devices, per_device(): lax.all_gather(fc2_weight, 'fsdp', axis=0, tiled=True)  42.7 us
    all_gather x1, waiting for transfers between devices, per_device(): lax.all_gather(fc1_weight, 'fsdp', axis=0, tiled=True)  42.6 us
  transfers between devices with their start and end apart: 17, of which 16 were waited for; matrix products, arithmetic and copies ran while one was open for 14% of the time, Pallas kernels for 0%

commit v1 on v0

--- a/solution.py
+++ b/solution.py
@@ -169,7 +169,9 @@
     partial_out = jnp.einsum(
         "te,de->td", attended, dense_full, preferred_element_type=jnp.float32
     ) + jnp.einsum("tf,df->td", hidden, fc2_full, preferred_element_type=jnp.float32)
-    summed = lax.psum(partial_out, "tp")
+    summed = partial_out
+    for hop in (1, 2):
+        summed = summed + lax.ppermute(summed, "tp", [(dev, dev ^ hop) for dev in range(4)])
     output = (inputs + summed + out_bias).astype(jnp.bfloat16)
     upstream_low = cotangent[0]
     upstream = upstream_low.astype(jnp.float32)

time: 1220 us -> 1110 us (0.910)
  waiting for transfers between devices: 942 us -> 844 us
    psum x1, waiting for transfers between devices: 291 us -> 189 us  [per_device(): full_grad = lax.psum(normed_grad, 'tp')]
    reduce_scatter x1, waiting for transfers between devices: 0.33 us -> 22.4 us  [per_device(): lax.psum_scatter(dense_grad, ('fsdp', 'ctx'), scatter_dimension=0, tiled=...]
    reduce_scatter x1, waiting for transfers between devices: 120 us -> 107 us  [per_device(): lax.psum_scatter(fc1_grad, ('fsdp', 'ctx'), scatter_dimension=0, tiled=True)]
    unnamed x103 -> x105, local copies, waits for them, and re-layouts: 26 us -> 24.3 us
  transfers between devices with their start and end apart: 17 -> 19, of which waited for: 16 -> 16; matrix products, arithmetic and copies ran while one was open for 14% -> 14% of each run, Pallas kernels for 0% -> 0%
where the time goes in v1:
time: 1110 us
  waiting for transfers between devices  844 us (76%)
  matrix products  110 us (10%)
  blocking collectives  63.1 us (6%)
  local copies, waits for them, and re-layouts  36.2 us (3%)
  other arithmetic  31.4 us (3%)
  between operations  15.6 us (1%)
    psum x1, waiting for transfers between devices, per_device(): full_grad = lax.psum(normed_grad, 'tp')  189 us
    reduce_scatter x1, waiting for transfers between devices, per_device(): lax.psum_scatter(fc2_grad, ('fsdp', 'ctx'), scatter_dimension=0, tiled=True)  110 us
    reduce_scatter x1, waiting for transfers between devices, per_device(): lax.psum_scatter(fc1_grad, ('fsdp', 'ctx'), scatter_dimension=0, tiled=True)  107 us
    reduce_scatter x1, waiting for transfers between devices, per_device(): lax.psum_scatter(qkv_grad, ('fsdp', 'ctx'), scatter_dimension=0, tiled=True)  78.6 us
    all_gather x1, waiting for transfers between devices, per_device(): lax.all_gather(reduced[3], 'ctx', axis=0, tiled=True)  58.1 us
    all_gather x1, waiting for transfers between devices, per_device(): lax.all_gather(reduced[2], 'ctx', axis=0, tiled=True)  53.5 us
    all_gather x1, waiting for transfers between devices, per_device(): lax.all_gather(fc2_weight, 'fsdp', axis=0, tiled=True)  42.7 us
    all_gather x1, waiting for transfers between devices, per_device(): lax.all_gather(fc1_weight, 'fsdp', axis=0, tiled=True)  42.6 us
  transfers between devices with their start and end apart: 19, of which 16 were waited for; matrix products, arithmetic and copies ran while one was open for 14% of the time, Pallas kernels for 0%

profile of v1, /device:TPU:0, one launch (start us, length us, event | category | flops | bytes accessed | tf_op | source)
XLA Modules:
  0.0 1105.3 jit_solution(8441367324626753058)
XLA Ops:
  7.3 2.7 copy.57
  11.0 6.2 all-gather.2
  17.2 5.5 all-gather.1
  24.5 34.9 %all-gather.19.cloned.1.call-done = bf16[2048,3,512]{0,2,1:T(8,128)(2,1)} async-done(((bf16[512,3,512]{0,2,1:T(8,128)(2,1)}), bf16[2048,3,512]{0,2,1:T(8,128)(2,1)}) %all-gather.19.cloned.1.call-update) | async-done | bytes 6291472 | tf_op jit(solution)/shard_map/all_gather | solution.py:84
  59.3 5.9 fusion.46
  68.0 15.5 %all-gather.23.cloned.1.call-done = bf16[2048,512]{1,0:T(8,128)(2,1)} async-done(((bf16[512,512]{1,0:T(8,128)(2,1)}), bf16[2048,512]{1,0:T(8,128)(2,1)}) %all-gather.23.cloned.1.call-update) | async-done | bytes 2097168 | tf_op jit(solution)/shard_map/all_gather | solution.py:85
  83.5 3.7 fusion.58
  87.2 2.1 slice.201
  89.4 17.5 %all-gather.21.cloned.1.call-done = bf16[1024,2,256]{0,2,1:T(8,128)(2,1)} async-done(((bf16[512,2,256]{0,2,1:T(8,128)(2,1)}), bf16[1024,2,256]{0,2,1:T(8,128)(2,1)}) %all-gather.21.cloned.1.call-update) | async-done | bytes 1048592 | tf_op jit(solution)/shard_map/all_gather | solution.py:132
  113.7 16.5 %all-gather.37.cloned.1.call-done = bf16[1024,1,2,256]{0,3,2,1:T(8,128)(2,1)} async-done(((bf16[512,1,2,256]{0,3,2,1:T(8,128)(2,1)}), bf16[1024,1,2,256]{0,3,2,1:T(8,128)(2,1)}) %all-gather.37.cloned.1.call-update) | async-done | bytes 1048592 | tf_op jit(solution)/shard_map/all_gather | solution.py:133
  130.2 2.5 multiply_reduce_fusion.2
  142.4 3.3 convolution_bitcast_fusion.1
  150.0 14.8 %reduce-scatter.9.cloned.1.call-done = f32[512,2,256]{2,0,1:T(8,128)} async-done(((f32[1024,2,256]{2,0,1:T(8,128)}), f32[512,2,256]{2,0,1:T(8,128)}) %reduce-scatter.9.cloned.1.call-update) | async-done | bytes 1048592 | tf_op jit(solution)/shard_map/reduce_scatter | solution.py:217
  164.8 2.1 convert.64
  166.9 2.2 copy.60
  171.1 28.3 %reduce-scatter.7.cloned.1.call-done = f32[512,2,256]{0,2,1:T(8,128)} async-done(((f32[1024,2,256]{0,2,1:T(8,128)}), f32[512,2,256]{0,2,1:T(8,128)}) %reduce-scatter.7.cloned.1.call-update) | async-done | bytes 1048592 | tf_op jit(solution)/shard_map/reduce_scatter | solution.py:216
  203.0 2.1 copy.61
  207.1 8.8 fusion.40
  216.7 42.6 %all-gather.25.cloned.1.call-done = bf16[2048,2048]{1,0:T(8,128)(2,1)} async-done(((bf16[512,2048]{1,0:T(8,128)(2,1)}), bf16[2048,2048]{1,0:T(8,128)(2,1)}) %all-gather.25.cloned.1.call-update) | async-done | bytes 8388624 | tf_op jit(solution)/shard_map/all_gather | solution.py:86
  259.3 17.2 %fusion.20 = (bf16[512,2048]{1,0:T(8,128)(2,1)}, f32[512,2048]{1,0:T(8,128)}) fusion(f32[2048]{0:T(1024)S(1)} %convert_element_type.135, bf16[2048,2048]{1,0:T(8,128)(2,1)} %all-gather.25.cloned.1.call-done, bf16[1,512,2048]{2,1,0:T(8,128)(2,1)S(1)} %copy-done.4, f32[2048]{0:T(1024)S(1)} %bitcast.223, f32[2048]{0:T(1024)S(1)} %bitcast.214, ...), kind=kOutput, calls=%fused_computation.27 | convolution fusion | flops 4370464768 | bytes 16805888 | tf_op jit(solution)/shard_map/dot_general | solution.py:165
  276.5 42.7 %all-gather.27.cloned.1.call-done = bf16[2048,2048]{1,0:T(8,128)(2,1)} async-done(((bf16[512,2048]{1,0:T(8,128)(2,1)}), bf16[2048,2048]{1,0:T(8,128)(2,1)}) %all-gather.27.cloned.1.call-update) | async-done | bytes 8388624 | tf_op jit(solution)/shard_map/all_gather | solution.py:87
  319.2 9.4 convert_reduce_fusion.2
  329.9 8.8 fusion.92
  339.2 12.5 %convolution_bitcast_fusion = f32[2048,2048]{0,1:T(8,128)} fusion(bf16[512,2048]{1,0:T(8,128)(2,1)} %get-tuple-element.102, bf16[1,512,2048]{2,1,0:T(8,128)(2,1)} %param.27), kind=kOutput, calls=%fused_computation | convolution fusion | flops 4294967296 | bytes 20971520 | tf_op jit(solution)/shard_map/td,tf->df/dot_general | solution.py:180
  351.8 22.4 %reduce-scatter.13.cloned.1.call-done = f32[256,512]{0,1:T(8,128)} async-done(((f32[2048,512]{0,1:T(8,128)}), f32[256,512]{0,1:T(8,128)}) %reduce-scatter.13.cloned.1.call-update) | async-done | bytes 524304 | tf_op jit(solution)/shard_map/reduce_scatter | solution.py:243
  374.3 7.7 fusion.100
  382.1 8.8 bitcast_add_fusion
  391.0 78.6 %reduce-scatter.11.cloned.1.call-done = f32[256,3,512]{2,0,1:T(8,128)} async-done(((f32[2048,3,512]{2,0,1:T(8,128)}), f32[256,3,512]{2,0,1:T(8,128)}) %reduce-scatter.11.cloned.1.call-update) | async-done | bytes 1572880 | tf_op jit(solution)/shard_map/reduce_scatter | solution.py:242
  469.8 7.8 fusion.99
  477.6 3.3 convolution_add_fusion
  482.4 107.0 %reduce-scatter.15.cloned.1.call-done = f32[256,2048]{1,0:T(8,128)} async-done(((f32[2048,2048]{1,0:T(8,128)}), f32[256,2048]{1,0:T(8,128)}) %reduce-scatter.15.cloned.1.call-update) | async-done | bytes 2097168 | tf_op jit(solution)/shard_map/reduce_scatter | solution.py:244
  589.7 6.6 add.207
  596.3 2.4 collective-permute-start.1
  598.8 110.1 %reduce-scatter.17.cloned.1.call-done = f32[256,2048]{0,1:T(8,128)} async-done(((f32[2048,2048]{0,1:T(8,128)}), f32[256,2048]{0,1:T(8,128)}) %reduce-scatter.17.cloned.1.call-update) | async-done | bytes 2097168 | tf_op jit(solution)/shard_map/reduce_scatter | solution.py:245
  710.2 5.2 all-gather.4
  715.4 5.2 all-gather.3
  721.9 9.8 all-gather.31.cloned.1.call-done
  731.7 2.5 copy.66
  734.2 188.9 %all-reduce.6.cloned.1.call-done = f32[512,2048]{1,0:T(8,128)} async-done(((f32[512,2048]{1,0:T(8,128)}), f32[512,2048]{1,0:T(8,128)}) %all-reduce.6.cloned.1.call-update) | async-done | bytes 4194320 | tf_op jit(solution)/shard_map/psum | solution.py:231
  923.1 3.8 fusion.13
  927.2 7.1 convert_reduce_fusion
  934.3 28.2 %all-reduce.3 = (f32[2048]{0:T(1024)S(1)}, f32[2048]{0:T(1024)S(1)}, f32[3,512]{1,0:T(4,128)}, f32[2048]{0:T(1024)S(1)}, f32[2048]{0:T(1024)}) all-reduce(f32[2048]{0:T(1024)S(1)} %get-tuple-element.60, f32[2048]{0:T(1024)S(1)} %get-tuple-element.63, ...), channel_id=5, replica_groups=mesh['fsdp'=4,'ctx'=2,'tp'=4] {'fsdp','ctx'}, use_global_device_ids=true, to_apply=%region_20.21.clone | all-reduce | flops 9728 | bytes 77824
  962.6 4.4 all-gather.7
  967.0 4.2 all-gather.5
  971.3 4.2 all-gather.6
  975.6 53.5 %all-gather.33.cloned.1.call-done = f32[512,2048]{1,0:T(8,128)} async-done(((f32[256,2048]{1,0:T(8,128)}), f32[512,2048]{1,0:T(8,128)}) %all-gather.33.cloned.1.call-update) | async-done | bytes 4194320 | tf_op jit(solution)/shard_map/all_gather | solution.py:253
  1029.1 58.1 %all-gather.35.cloned.1.call-done = f32[512,2048]{0,1:T(8,128)} async-done(((f32[256,2048]{0,1:T(8,128)}), f32[512,2048]{0,1:T(8,128)}) %all-gather.35.cloned.1.call-update) | async-done | bytes 4194320 | tf_op jit(solution)/shard_map/all_gather | solution.py:254
  1087.2 5.3 copy.67
  (198 shorter events, 46.6 us)
Async XLA Ops:
  7.2 3.7 copy-start.35
  7.2 3.8 copy-start.36
  7.2 3.8 copy-start.37
  7.2 15.5 %copy-start.33 = (bf16[3,512]{1,0:T(4,128)(2,1)S(1)}, bf16[3,512]{1,0:T(4,128)(2,1)}, u32[]{:S(2)}) copy-start(bf16[3,512]{1,0:T(4,128)(2,1)} %param.20) | copy-start | bytes 9220
  7.2 15.5 %copy-start.40 = (s32[1,3]{1,0:T(1,128)S(1)}, s32[1,3]{1,0:T(1,128)}, u32[]{:S(2)}) copy-start(s32[1,3]{1,0:T(1,128)} %param.15) | copy-start | bytes 40
  7.2 15.8 %copy-start.3 = (bf16[1,512,2048]{2,1,0:T(8,128)(2,1)S(1)}, bf16[1,512,2048]{2,1,0:T(8,128)(2,1)}, u32[]{:S(2)}) copy-start(bf16[1,512,2048]{2,1,0:T(8,128)(2,1)} %param.14) | copy-start | bytes 6291460
  7.2 52.1 %all-gather.19.cloned.1.call-start = ((), (), s32[]{:S(2)}) async-start(), calls=%async_computation.6 | async-start | bytes 7864320 | tf_op jit(solution)/shard_map/all_gather | solution.py:84
  10.0 73.5 %all-gather.23.cloned.1.call-start = ((), (), s32[]{:S(2)}) async-start(), calls=%async_computation.8 | async-start | bytes 2621440 | tf_op jit(solution)/shard_map/all_gather | solution.py:85
  10.8 96.1 %all-gather.21.cloned.1.call-start = ((), (), s32[]{:S(2)}) async-start(), calls=%async_computation.7 | async-start | bytes 1572864 | tf_op jit(solution)/shard_map/all_gather | solution.py:132
  17.2 48.0 %copy-start.31 = (f32[4,1,512]{2,1,0:T(1,128)}, f32[4,1,512]{2,1,0:T(1,128)S(1)}, u32[]{:S(2)}) copy-start(f32[4,1,512]{2,1,0:T(1,128)S(1)} %convert_element_type.153) | copy-start | bytes 24580
  24.4 41.1 %copy-start.27 = (f32[512,32]{0,1:T(8,128)}, f32[512,32]{0,1:T(8,128)S(1)}, u32[]{:S(2)}) copy-start(f32[512,32]{0,1:T(8,128)S(1)} %get-tuple-element.90) | copy-start | bytes 196612
  24.4 41.1 %copy-start.28 = (f32[512,32]{0,1:T(8,128)}, f32[512,32]{0,1:T(8,128)S(1)}, u32[]{:S(2)}) copy-start(f32[512,32]{0,1:T(8,128)S(1)} %get-tuple-element.91) | copy-start | bytes 196612
  65.3 18.2 %copy-start.6 = (bf16[1,512,2048]{2,1,0:T(8,128)(2,1)S(1)}, bf16[1,512,2048]{2,1,0:T(8,128)(2,1)}, u32[]{:S(2)}) copy-start(bf16[1,512,2048]{2,1,0:T(8,128)(2,1)} %param.27) | copy-start | bytes 6291460
  67.8 62.4 %all-gather.37.cloned.1.call-start = ((), (), s32[]{:S(2)}) async-start(), calls=%async_computation.22 | async-start | bytes 1572864 | tf_op jit(solution)/shard_map/all_gather | solution.py:133
  68.0 73.5 %copy-start.29 = (f32[512]{0:T(512)}, f32[512]{0:T(512)S(1)}, u32[]{:S(2)}) copy-start(f32[512]{0:T(512)S(1)} %get-tuple-element.93) | copy-start | bytes 6148
  89.3 75.5 %reduce-scatter.9.cloned.1.call-start = ((), (), s32[]{:S(2)}) async-start(), calls=%async_computation.12 | async-start | bytes 3145728 | tf_op jit(solution)/shard_map/reduce_scatter | solution.py:217
  113.5 85.9 %reduce-scatter.7.cloned.1.call-start = ((), (), s32[]{:S(2)}) async-start(), calls=%async_computation.11 | async-start | bytes 3145728 | tf_op jit(solution)/shard_map/reduce_scatter | solution.py:216
  130.2 2.5 copy-start.1
  137.6 121.7 %all-gather.25.cloned.1.call-start = ((), (), s32[]{:S(2)}) async-start(), calls=%async_computation.9 | async-start | bytes 10485760 | tf_op jit(solution)/shard_map/all_gather | solution.py:86
  138.3 180.8 %all-gather.27.cloned.1.call-start = ((), (), s32[]{:S(2)}) async-start(), calls=%async_computation.10 | async-start | bytes 10485760 | tf_op jit(solution)/shard_map/all_gather | solution.py:87
  139.1 235.1 %reduce-scatter.13.cloned.1.call-start = ((), (), s32[]{:S(2)}) async-start(), calls=%async_computation.16 | async-start | bytes 4718592 | tf_op jit(solution)/shard_map/reduce_scatter | solution.py:243
  142.4 3.4 copy-start.11
  145.8 323.9 %reduce-scatter.11.cloned.1.call-start = ((), (), s32[]{:S(2)}) async-start(), calls=%async_computation.14 | async-start | bytes 14155776 | tf_op jit(solution)/shard_map/reduce_scatter | solution.py:242
  166.9 40.2 %copy-start.4 = (bf16[1,512,2048]{2,1,0:T(8,128)(2,1)S(1)}, bf16[1,512,2048]{2,1,0:T(8,128)(2,1)}, u32[]{:S(2)}) copy-start(bf16[1,512,2048]{2,1,0:T(8,128)(2,1)} %param.14) | copy-start | bytes 6291460
  216.0 43.3 %copy-start.32 = (f32[4,1,512]{2,1,0:T(1,128)S(1)}, f32[4,1,512]{2,1,0:T(1,128)}, u32[]{:S(2)}) copy-start(f32[4,1,512]{2,1,0:T(1,128)} %copy-done.31) | copy-start | bytes 24580
  216.0 373.4 %reduce-scatter.15.cloned.1.call-start = ((), (), s32[]{:S(2)}) async-start(), calls=%async_computation.18 | async-start | bytes 18874368 | tf_op jit(solution)/shard_map/reduce_scatter | solution.py:244
  338.7 370.1 %reduce-scatter.17.cloned.1.call-start = ((), (), s32[]{:S(2)}) async-start(), calls=%async_computation.20 | async-start | bytes 18874368 | tf_op jit(solution)/shard_map/reduce_scatter | solution.py:245
  351.7 380.0 %all-gather.31.cloned.1.call-start = ((), (), s32[]{:S(2)}) async-start(), calls=%async_computation.17 | async-start | bytes 1572864 | tf_op jit(solution)/shard_map/all_gather | solution.py:252
  374.2 548.9 %all-reduce.6.cloned.1.call-start = ((), (), s32[]{:S(2)}) async-start(), calls=%async_computation.13 | async-start | bytes 8388608 | tf_op jit(solution)/shard_map/psum | solution.py:231
  374.3 7.8 copy-start.17
  374.3 7.8 copy-start.19
  374.3 7.8 copy-start.21
  390.9 78.8 %copy-start.30 = (f32[512]{0:T(512)S(1)}, f32[512]{0:T(512)}, u32[]{:S(2)}) copy-start(f32[512]{0:T(512)} %copy-done.29) | copy-start | bytes 6148
  390.9 584.6 %all-gather.29.cloned.1.call-start = ((), (), s32[]{:S(2)}) async-start(), calls=%async_computation.15 | async-start | bytes 4718592 | tf_op jit(solution)/shard_map/all_gather | solution.py:251
  469.6 559.4 %all-gather.33.cloned.1.call-start = ((), (), s32[]{:S(2)}) async-start(), calls=%async_computation.19 | async-start | bytes 6291456 | tf_op jit(solution)/shard_map/all_gather | solution.py:253
  469.8 7.8 copy-start.24
  481.0 108.8 %collective-permute-start = (f32[512,2048]{1,0:T(8,128)}, f32[512,2048]{1,0:T(8,128)}, u32[]{:S(2)}, u32[]{:S(2)}) collective-permute-start(f32[512,2048]{1,0:T(8,128)} %convolution_add_fusion), channel_id=1, source_target_pairs={{0,1},{1,0},{2,3},{3,2},{4,5},{5,4},{6,7},{7,6},{8,9},{9,8},{10,11... | collective-permute-start | bytes 12582920 | tf_op jit(solution)/shard_map/ppermute | solution.py:174
  589.4 119.4 %copy-start.38 = (bf16[512]{0:T(512)(128)(2,1)S(1)}, bf16[512]{0:T(512)(128)(2,1)}, u32[]{:S(2)}) copy-start(bf16[512]{0:T(512)(128)(2,1)} %param.22) | copy-start | bytes 3076
  589.4 119.5 %copy-start.39 = (bf16[512]{0:T(512)(128)(2,1)S(1)}, bf16[512]{0:T(512)(128)(2,1)}, u32[]{:S(2)}) copy-start(bf16[512]{0:T(512)(128)(2,1)} %param.26) | copy-start | bytes 3076
  589.5 119.5 %copy-start.42 = (u32[32]{0:T(128)S(1)}, u32[32]{0:T(128)}, u32[]{:S(2)}) copy-start(u32[32]{0:T(128)} %constant.160) | copy-start | bytes 388
  589.5 131.1 %copy-start.18 = (bf16[512,1,512]{2,0,1:T(8,128)(2,1)S(1)}, bf16[512,1,512]{2,0,1:T(8,128)(2,1)}, u32[]{:S(2)}) copy-start(bf16[512,1,512]{2,0,1:T(8,128)(2,1)} %copy.63) | copy-start | bytes 1572868
  589.5 131.1 %copy-start.20 = (bf16[512,1,512]{2,0,1:T(8,128)(2,1)S(1)}, bf16[512,1,512]{2,0,1:T(8,128)(2,1)}, u32[]{:S(2)}) copy-start(bf16[512,1,512]{2,0,1:T(8,128)(2,1)} %copy.61) | copy-start | bytes 1572868
  589.5 497.7 %all-gather.35.cloned.1.call-start = ((), (), s32[]{:S(2)}) async-start(), calls=%async_computation.21 | async-start | bytes 6291456 | tf_op jit(solution)/shard_map/all_gather | solution.py:254
  596.3 330.6 %collective-permute-start.1 = (f32[512,2048]{1,0:T(8,128)}, f32[512,2048]{1,0:T(8,128)}, u32[]{:S(2)}, u32[]{:S(2)}) collective-permute-start(f32[512,2048]{1,0:T(8,128)} %add.207), channel_id=1, source_target_pairs={{0,2},{1,3},{2,0},{3,1},{4,6},{5,7},{6,4},{7,5},{8,10},{9,11},{10,... | collective-permute-start | bytes 12582920 | tf_op jit(solution)/shard_map/ppermute | solution.py:174
  923.1 3.8 copy-start.5
  923.1 4.1 copy-start.8
  975.6 118.7 %copy-start.14 = (f32[512,3,512]{2,0,1:T(8,128)S(1)}, f32[512,3,512]{2,0,1:T(8,128)}, u32[]{:S(2)}) copy-start(f32[512,3,512]{2,0,1:T(8,128)} %all-gather.29.cloned.1.call-done) | copy-start | bytes 9437188
  1092.6 4.0 copy-start.9
  (15 other events, 22.3 us)
Sparse Core Ops, SparseCore 0:
  10.2 49.1 all-gather.18
  60.9 22.5 all-gather.22
  85.6 21.2 all-gather.20
  108.9 21.2 all-gather.36
  132.9 31.8 reduce-scatter.8
  167.5 31.8 reduce-scatter.6
  201.0 58.2 all-gather.24
  260.9 58.2 all-gather.26
  323.1 51.0 reduce-scatter.12
  377.5 92.0 reduce-scatter.10
  473.2 116.1 reduce-scatter.14
  592.8 115.9 reduce-scatter.16
  710.4 21.2 all-gather.30
  734.5 188.5 all-reduce.5
  924.5 46.3 all-gather.28
  972.3 56.7 all-gather.32
  1030.5 56.7 all-gather.34
